TPU v7x, 256 devices: a whole 4x4x8 slice. The times are simulated.
256 devices in a mesh: row: 16 (over z, core), col: 16 (over y, x).
Axes of the slice: x: 4, y: 4, z: 8, core: 2. Of those that a mesh axis runs over, the one named last changes fastest.
Arguments:
- start_basis: float32 [32, 131072], P(None, ('row', 'col')), may hold values from -6 to 6
- degrees: float32 [131072], P(('row', 'col')), may hold values from 0.5 to 1.5
- tiles: float32 [8192, 256, 256], P(('row', 'col')), may hold values from -0.046875 to 0.046875
- tile_rows: int32 [16, 512], P('row', 'col'), may hold values from 0 to 31, as said below
- tile_cols: int32 [16, 512], P('row', 'col'), may hold values from 0 to 31
- counts: int32 [16, 16], P('row', 'col'), may hold values from 1 to 31, as said below
Outputs:
- basis: float32 [32, 131072], P(None, ('row', 'col'))
- projected: float32 [32, 32], replicated
Inputs may be any that keep to these rules, and one draw needn't show every extreme that they name: `tile_rows`: the 32 (row, column) pairs of one device are distinct. counts[r, c] + counts[r', c] <= 32 where r' differs from r by 8; equality holds in column 0.
All inputs are finite; a program needn't handle non-finite values.
Results may differ from a plain program's by a relative error of at most 0.0003.
Values sent between devices are 32-bit elements; how exact they have to be, the bound alone decides.
A program may use at most 64 MiB of HBM per device.

v0:
```python
import jax
import jax.numpy as jnp
from jax import lax
from jax.sharding import PartitionSpec as P

DEGREE = 3
center_shift = 1.0
spread_radius = 1.4
group_width = 8


def tile_products(blocks, tiles, row_local, col_local, live, row_blocks):
    subspace = blocks.shape[0]
    edge = blocks.shape[2]
    block_ids = jnp.arange(row_blocks, dtype=jnp.int32)

    def add_group(index, total):
        start = index * group_width
        group_tiles = lax.dynamic_slice_in_dim(tiles, start, group_width, 0)
        group_rows = lax.dynamic_slice_in_dim(row_local, start, group_width, 0)
        group_cols = lax.dynamic_slice_in_dim(col_local, start, group_width, 0)
        picked = jnp.take(blocks, group_cols, axis=1)
        product = jnp.einsum("kgj,gij->kgi", picked, group_tiles, precision=lax.Precision.HIGHEST)
        valid = start + jnp.arange(group_width, dtype=jnp.int32) < live
        select = ((group_rows[None, :] == block_ids[:, None]) & valid[None, :]).astype(jnp.float32)
        return total + jnp.einsum("ig,kgb->kib", select, product, precision=lax.Precision.HIGHEST)

    initial = jnp.zeros((subspace, row_blocks, edge), jnp.float32)
    return lax.fori_loop(0, (live + group_width - 1) // group_width, add_group, initial)


def inner_products(left, right):
    return jnp.einsum("kn,mn->km", left, right, precision=lax.Precision.HIGHEST)


def body(start_basis, degrees, tiles, tile_rows, tile_cols, counts):
    subspace = start_basis.shape[0]
    edge = tiles.shape[1]
    row_local = tile_rows[0]
    col_local = tile_cols[0]
    live_count = counts[0, 0]
    row_blocks = lax.axis_size("col") * start_basis.shape[1] // edge
    nverts = lax.axis_size("row") * lax.axis_size("col") * start_basis.shape[1]

    def apply_operator(vectors):
        gathered = lax.all_gather(vectors, "row", axis=1, tiled=True)
        blocks = gathered.reshape(subspace, -1, edge)
        partial_value = tile_products(blocks, tiles, row_local, col_local, live_count, row_blocks)
        summed = lax.psum_scatter(
            partial_value.reshape(subspace, -1), "col", scatter_dimension=1, tiled=True
        )
        return degrees[None, :] * vectors - summed

    def shifted(vectors):
        return (apply_operator(vectors) - center_shift * vectors) / spread_radius

    previous = start_basis
    filtered = shifted(start_basis)
    for level in range(DEGREE - 1):
        following = 2.0 * shifted(filtered) - previous
        previous, filtered = (filtered, following)
    gram_matrix = lax.psum(inner_products(filtered, filtered), ("row", "col")) / nverts
    factor = jnp.linalg.cholesky(gram_matrix)
    basis = jax.scipy.linalg.solve_triangular(factor, filtered, lower=True)
    image = apply_operator(basis)
    moment = lax.psum(inner_products(basis, image), ("row", "col")) / nverts
    projected = 0.5 * (moment + moment.T)
    return (basis, projected)


def solution(mesh):
    return jax.shard_map(
        body,
        mesh=mesh,
        in_specs=(
            P(None, ("row", "col")),
            P(("row", "col")),
            P(("row", "col"), None, None),
            P("row", "col"),
            P("row", "col"),
            P("row", "col"),
        ),
        out_specs=(P(None, ("row", "col")), P()),
        check_vma=False,
    )
```

profile of v0, /device:TPU:1, one launch (start us, length us, event | category | flops | bytes accessed | tf_op | source)
XLA Modules:
  0.0 776.5 jit_solution(2379847340742066916)
XLA Ops:
  8.6 44.0 %all-gather.5.cloned.1.call-done = f32[32,8192]{1,0:T(8,128)} async-done(((f32[32,512]{1,0:T(8,128)}), f32[32,8192]{1,0:T(8,128)}) %all-gather.5.cloned.1.call-update) | async-done | bytes 1048592 | tf_op jit(solution)/shard_map/all_gather | solution.py:46
  54.1 29.0 %while.44 = (s32[]{:T(128)}, f32[32,32,256]{2,1,0:T(8,128)S(1)}, s32[]{:T(128)}, f32[32,256,256]{2,1,0:T(8,128)}, s32[32]{0:T(128)}, /*index=5*/f32[32,32,256]{2...) while((s32[]{:T(128)}, f32[32,32,256]{2,1,0:T(8,128)S(1)}, ...), condition=%wide.region_1.3_spmd.clone, body=%wide.region_0.2_spmd.clone.sunk | while | flops 226821696 | bytes 5509559 | solution.py:29
  56.1 3.6 fusion.122
  63.4 3.6 fusion.122
  70.6 3.6 fusion.122
  77.9 3.6 fusion.122
  84.8 75.6 %reduce-scatter.5.cloned.1.call-done = f32[32,512]{1,0:T(8,128)} async-done(((f32[32,8192]{1,0:T(8,128)}), f32[32,512]{1,0:T(8,128)}) %reduce-scatter.5.cloned.1.call-update) | async-done | bytes 65552 | tf_op jit(solution)/shard_map/reduce_scatter | solution.py:49
  161.9 41.0 %all-gather.7.cloned.1.call-done = f32[32,8192]{1,0:T(8,128)} async-done(((f32[32,512]{1,0:T(8,128)}), f32[32,8192]{1,0:T(8,128)}) %all-gather.7.cloned.1.call-update) | async-done | bytes 1048592 | tf_op jit(solution)/shard_map/all_gather | solution.py:46
  204.4 29.0 %while.45 = (s32[]{:T(128)}, f32[32,32,256]{2,1,0:T(8,128)S(1)}, s32[]{:T(128)}, f32[32,256,256]{2,1,0:T(8,128)}, s32[32]{0:T(128)}, /*index=5*/f32[32,32,256]{2...) while((s32[]{:T(128)}, f32[32,32,256]{2,1,0:T(8,128)S(1)}, ...), condition=%wide.region_4.6_spmd.clone, body=%wide.region_3.5_spmd.clone.sunk | while | flops 226821696 | bytes 5509559 | solution.py:29
  206.4 3.6 fusion.128
  213.6 3.6 fusion.128
  220.9 3.6 fusion.128
  228.1 3.6 fusion.128
  235.1 75.6 %reduce-scatter.7.cloned.1.call-done = f32[32,512]{1,0:T(8,128)} async-done(((f32[32,8192]{1,0:T(8,128)}), f32[32,512]{1,0:T(8,128)}) %reduce-scatter.7.cloned.1.call-update) | async-done | bytes 65552 | tf_op jit(solution)/shard_map/reduce_scatter | solution.py:49
  312.3 40.8 %all-gather.9.cloned.1.call-done = f32[32,8192]{1,0:T(8,128)} async-done(((f32[32,512]{1,0:T(8,128)}), f32[32,8192]{1,0:T(8,128)}) %all-gather.9.cloned.1.call-update) | async-done | bytes 1048592 | tf_op jit(solution)/shard_map/all_gather | solution.py:46
  354.6 29.0 %while.46 = (s32[]{:T(128)}, f32[32,32,256]{2,1,0:T(8,128)S(1)}, s32[]{:T(128)}, f32[32,256,256]{2,1,0:T(8,128)}, s32[32]{0:T(128)}, /*index=5*/f32[32,32,256]{2...) while((s32[]{:T(128)}, f32[32,32,256]{2,1,0:T(8,128)S(1)}, ...), condition=%wide.region_7.9_spmd.clone, body=%wide.region_6.8_spmd.clone.sunk | while | flops 226821696 | bytes 5509559 | solution.py:29
  356.6 3.6 fusion.134
  363.8 3.6 fusion.134
  371.1 3.6 fusion.134
  378.3 3.6 fusion.134
  385.3 75.6 %reduce-scatter.9.cloned.1.call-done = f32[32,512]{1,0:T(8,128)} async-done(((f32[32,8192]{1,0:T(8,128)}), f32[32,512]{1,0:T(8,128)}) %reduce-scatter.9.cloned.1.call-update) | async-done | bytes 65552 | tf_op jit(solution)/shard_map/reduce_scatter | solution.py:49
  462.0 77.5 %psum.14 = f32[32,32]{0,1:T(8,128)S(1)} all-reduce(f32[32,32]{0,1:T(8,128)S(1)} %fusion.89), channel_id=1, replica_groups=mesh['row'=16,'col'=16] {'row','col'}, use_global_device_ids=true, to_apply=%region_9.11 | all-reduce | flops 1024 | bytes 8192 | tf_op jit(solution)/shard_map/psum | solution.py:62
  539.6 2.9 cholesky.16
  543.9 2.4 custom-call.7
  547.3 35.6 %all-gather.11.cloned.1.call-done = f32[32,8192]{1,0:T(8,128)} async-done(((f32[32,512]{1,0:T(8,128)}), f32[32,8192]{1,0:T(8,128)}) %all-gather.11.cloned.1.call-update) | async-done | bytes 1048592 | tf_op jit(solution)/shard_map/all_gather | solution.py:46
  584.4 29.0 %while.47 = (s32[]{:T(128)}, f32[32,32,256]{2,1,0:T(8,128)S(1)}, s32[]{:T(128)}, f32[32,256,256]{2,1,0:T(8,128)}, s32[32]{0:T(128)}, /*index=5*/f32[32,32,256]{2...) while((s32[]{:T(128)}, f32[32,32,256]{2,1,0:T(8,128)S(1)}, ...), condition=%wide.region_13.15_spmd.clone, body=%wide.region_12.14_spmd.clone.sunk | while | flops 226821696 | bytes 5509559 | solution.py:29
  586.4 3.6 fusion.140
  593.6 3.6 fusion.140
  600.9 3.6 fusion.140
  608.1 3.6 fusion.140
  615.0 75.7 %reduce-scatter.11.cloned.1.call-done = f32[32,512]{1,0:T(8,128)} async-done(((f32[32,8192]{1,0:T(8,128)}), f32[32,512]{1,0:T(8,128)}) %reduce-scatter.11.cloned.1.call-update) | async-done | bytes 65552 | tf_op jit(solution)/shard_map/reduce_scatter | solution.py:49
  691.7 77.3 %psum.15 = f32[32,32]{0,1:T(8,128)S(1)} all-reduce(f32[32,32]{0,1:T(8,128)S(1)} %fusion.80), channel_id=1, replica_groups=mesh['row'=16,'col'=16] {'row','col'}, use_global_device_ids=true, to_apply=%region_15.17 | all-reduce | flops 1024 | bytes 8192 | tf_op jit(solution)/shard_map/psum | solution.py:66
  (136 shorter events, 78.6 us)
Async XLA Ops:
  7.2 45.4 %all-gather.5.cloned.1.call-start = ((), (), s32[]{:S(2)}) async-start(), calls=%async_computation.4 | async-start | bytes 1114112 | tf_op jit(solution)/shard_map/all_gather | solution.py:46
  7.9 152.5 %reduce-scatter.5.cloned.1.call-start = ((), (), s32[]{:S(2)}) async-start(), calls=%async_computation.5 | async-start | bytes 1114112 | tf_op jit(solution)/shard_map/reduce_scatter | solution.py:49
  54.1 106.3 %copy-start = (f32[32,512]{1,0:T(8,128)S(1)}, f32[32,512]{1,0:T(8,128)}, u32[]{:S(2)}) copy-start(f32[32,512]{1,0:T(8,128)} %param.16) | copy-start | bytes 196612
  54.1 106.3 %copy-start.4 = (f32[512]{0:T(512)S(1)}, f32[512]{0:T(512)}, u32[]{:S(2)}) copy-start(f32[512]{0:T(512)} %param.17) | copy-start | bytes 6148
  84.7 118.2 %all-gather.7.cloned.1.call-start = ((), (), s32[]{:S(2)}) async-start(), calls=%async_computation.6 | async-start | bytes 1114112 | tf_op jit(solution)/shard_map/all_gather | solution.py:46
  161.9 148.8 %reduce-scatter.7.cloned.1.call-start = ((), (), s32[]{:S(2)}) async-start(), calls=%async_computation.7 | async-start | bytes 1114112 | tf_op jit(solution)/shard_map/reduce_scatter | solution.py:49
  204.4 106.3 %copy-start.2 = (f32[32,512]{1,0:T(8,128)S(1)}, f32[32,512]{1,0:T(8,128)}, u32[]{:S(2)}) copy-start(f32[32,512]{1,0:T(8,128)} %reduce-scatter.5.cloned.1.call-done) | copy-start | bytes 196612
  235.0 118.1 %all-gather.9.cloned.1.call-start = ((), (), s32[]{:S(2)}) async-start(), calls=%async_computation.8 | async-start | bytes 1114112 | tf_op jit(solution)/shard_map/all_gather | solution.py:46
  312.2 148.7 %reduce-scatter.9.cloned.1.call-start = ((), (), s32[]{:S(2)}) async-start(), calls=%async_computation.9 | async-start | bytes 1114112 | tf_op jit(solution)/shard_map/reduce_scatter | solution.py:49
  354.6 106.3 %copy-start.3 = (f32[32,512]{1,0:T(8,128)S(1)}, f32[32,512]{1,0:T(8,128)}, u32[]{:S(2)}) copy-start(f32[32,512]{1,0:T(8,128)} %multiply_subtract_fusion.1) | copy-start | bytes 196612
  385.2 197.7 %all-gather.11.cloned.1.call-start = ((), (), s32[]{:S(2)}) async-start(), calls=%async_computation.10 | async-start | bytes 1114112 | tf_op jit(solution)/shard_map/all_gather | solution.py:46
  547.2 143.5 %reduce-scatter.11.cloned.1.call-start = ((), (), s32[]{:S(2)}) async-start(), calls=%async_computation.11 | async-start | bytes 1114112 | tf_op jit(solution)/shard_map/reduce_scatter | solution.py:49
  584.4 106.3 %copy-start.1 = (f32[32,512]{1,0:T(8,128)S(1)}, f32[32,512]{1,0:T(8,128)}, u32[]{:S(2)}) copy-start(f32[32,512]{1,0:T(8,128)} %fusion.87) | copy-start | bytes 196612
Sparse Core Ops, SparseCore 0:
  9.8 42.7 all-gather.4
  84.9 75.4 reduce-scatter.4
  162.8 40.0 all-gather.6
  235.1 75.5 reduce-scatter.6
  313.0 40.0 all-gather.8
  385.3 75.5 reduce-scatter.8
  547.4 35.5 all-gather.10
  615.1 75.4 reduce-scatter.10
where the time goes:
time: 778 us; the launch traced here: 777 us
  waiting for transfers between devices  465 us (60%)
  blocking collectives  155 us (20%)
  matrix products  74.3 us (10%)
  other arithmetic  33.4 us (4%)
  local copies, waits for them, and re-layouts  33.2 us (4%)
  between operations  15 us (2%)
    reduce_scatter x4, waiting for transfers between devices, apply_operator(): lax.psum_scatter(partial_value.reshape(subspace, -1), 'col', scatter_dime...  303 us
    all_gather x4, waiting for transfers between devices, apply_operator(): gathered = lax.all_gather(vectors, 'row', axis=1, tiled=True)  161 us
    psum x1, blocking collectives, body(): lax.psum(inner_products(filtered, filtered), ('row', 'col')) / nverts  77.5 us
    psum x1, blocking collectives, body(): moment = lax.psum(inner_products(basis, image), ('row', 'col')) / nverts  77.3 us
    dot_general x16, matrix products, add_group(): jnp.einsum('kgj,gij->kgi', picked, group_tiles, precision=lax.Precision.H...  58.1 us
    and x16, other arithmetic, add_group(): picked = jnp.take(blocks, group_cols, axis=1)  22.1 us
  transfers between devices with their start and end apart: 8, of which 8 were waited for; matrix products, arithmetic and copies ran while one was open for 0% of the time, Pallas kernels for 0%

commit v1 on v0

--- a/solution.py
+++ b/solution.py
@@ -59,7 +59,9 @@
     for level in range(DEGREE - 1):
         following = 2.0 * shifted(filtered) - previous
         previous, filtered = (filtered, following)
-    gram_matrix = lax.psum(inner_products(filtered, filtered), ("row", "col")) / nverts
+    gram_matrix = (
+        jnp.sum(lax.all_gather(inner_products(filtered, filtered), ("row", "col")), axis=0) / nverts
+    )
     factor = jnp.linalg.cholesky(gram_matrix)
     basis = jax.scipy.linalg.solve_triangular(factor, filtered, lower=True)
     image = apply_operator(basis)

time: 778 us -> 819 us (1.053)
  waiting for transfers between devices: 465 us -> 585 us
  blocking collectives: 155 us -> 77.3 us
    all_gather x0 -> x1, waiting for transfers between devices: none -> 120 us  [body(): lax.all_gather(inner_products(filtered, filtered), ('row', 'col'))]
    psum x1 -> x0, blocking collectives: 77.5 us -> none  [body(): lax.psum(inner_products(filtered, filtered), ('row', 'col')) / nverts]
  transfers between devices with their start and end apart: 8 -> 9, of which waited for: 8 -> 9; matrix products, arithmetic and copies ran while one was open for 0% -> 0% of each run, Pallas kernels for 0% -> 0%
where the time goes in v1:
time: 819 us; the launch traced here: 817 us
  waiting for transfers between devices  585 us (71%)
  blocking collectives  77.3 us (9%)
  matrix products  74.9 us (9%)
  other arithmetic  33.3 us (4%)
  local copies, waits for them, and re-layouts  30.5 us (4%)
  between operations  14.7 us (2%)
    reduce_scatter x4, waiting for transfers between devices, apply_operator(): lax.psum_scatter(partial_value.reshape(subspace, -1), 'col', scatter_dime...  303 us
    all_gather x4, waiting for transfers between devices, apply_operator(): gathered = lax.all_gather(vectors, 'row', axis=1, tiled=True)  162 us
    all_gather x1, waiting for transfers between devices, body(): lax.all_gather(inner_products(filtered, filtered), ('row', 'col'))  120 us
    psum x1, blocking collectives, body(): moment = lax.psum(inner_products(basis, image), ('row', 'col')) / nverts  77.3 us
    dot_general x16, matrix products, add_group(): jnp.einsum('kgj,gij->kgi', picked, group_tiles, precision=lax.Precision.H...  58.1 us
    and x16, other arithmetic, add_group(): picked = jnp.take(blocks, group_cols, axis=1)  19.5 us
  transfers between devices with their start and end apart: 9, of which 9 were waited for; matrix products, arithmetic and copies ran while one was open for 0% of the time, Pallas kernels for 0%

profile of v1, /device:TPU:1, one launch (start us, length us, event | category | flops | bytes accessed | tf_op | source)
XLA Modules:
  0.0 817.0 jit_solution(11961103311568205321)
XLA Ops:
  8.6 44.0 %all-gather.7.cloned.1.call-done = f32[32,8192]{1,0:T(8,128)} async-done(((f32[32,512]{1,0:T(8,128)}), f32[32,8192]{1,0:T(8,128)}) %all-gather.7.cloned.1.call-update) | async-done | bytes 1048592 | tf_op jit(solution)/shard_map/all_gather | solution.py:46
  54.1 29.0 %while.44 = (s32[]{:T(128)}, f32[32,32,256]{2,1,0:T(8,128)S(1)}, s32[]{:T(128)}, f32[32,256,256]{2,1,0:T(8,128)}, s32[32]{0:T(128)}, /*index=5*/f32[32,32,256]{2...) while((s32[]{:T(128)}, f32[32,32,256]{2,1,0:T(8,128)S(1)}, ...), condition=%wide.region_1.3_spmd.clone, body=%wide.region_0.2_spmd.clone.sunk | while | flops 226821696 | bytes 5509559 | solution.py:29
  56.1 3.6 fusion.123
  63.4 3.6 fusion.123
  70.6 3.6 fusion.123
  77.9 3.6 fusion.123
  84.8 75.6 %reduce-scatter.5.cloned.1.call-done = f32[32,512]{1,0:T(8,128)} async-done(((f32[32,8192]{1,0:T(8,128)}), f32[32,512]{1,0:T(8,128)}) %reduce-scatter.5.cloned.1.call-update) | async-done | bytes 65552 | tf_op jit(solution)/shard_map/reduce_scatter | solution.py:49
  161.9 41.0 %all-gather.9.cloned.1.call-done = f32[32,8192]{1,0:T(8,128)} async-done(((f32[32,512]{1,0:T(8,128)}), f32[32,8192]{1,0:T(8,128)}) %all-gather.9.cloned.1.call-update) | async-done | bytes 1048592 | tf_op jit(solution)/shard_map/all_gather | solution.py:46
  204.4 29.0 %while.45 = (s32[]{:T(128)}, f32[32,32,256]{2,1,0:T(8,128)S(1)}, s32[]{:T(128)}, f32[32,256,256]{2,1,0:T(8,128)}, s32[32]{0:T(128)}, /*index=5*/f32[32,32,256]{2...) while((s32[]{:T(128)}, f32[32,32,256]{2,1,0:T(8,128)S(1)}, ...), condition=%wide.region_4.6_spmd.clone, body=%wide.region_3.5_spmd.clone.sunk | while | flops 226821696 | bytes 5509559 | solution.py:29
  206.4 3.6 fusion.129
  213.6 3.6 fusion.129
  220.9 3.6 fusion.129
  228.2 3.6 fusion.129
  235.1 75.6 %reduce-scatter.7.cloned.1.call-done = f32[32,512]{1,0:T(8,128)} async-done(((f32[32,8192]{1,0:T(8,128)}), f32[32,512]{1,0:T(8,128)}) %reduce-scatter.7.cloned.1.call-update) | async-done | bytes 65552 | tf_op jit(solution)/shard_map/reduce_scatter | solution.py:49
  312.3 40.8 %all-gather.11.cloned.1.call-done = f32[32,8192]{1,0:T(8,128)} async-done(((f32[32,512]{1,0:T(8,128)}), f32[32,8192]{1,0:T(8,128)}) %all-gather.11.cloned.1.call-update) | async-done | bytes 1048592 | tf_op jit(solution)/shard_map/all_gather | solution.py:46
  354.6 29.0 %while.46 = (s32[]{:T(128)}, f32[32,32,256]{2,1,0:T(8,128)S(1)}, s32[]{:T(128)}, f32[32,256,256]{2,1,0:T(8,128)}, s32[32]{0:T(128)}, /*index=5*/f32[32,32,256]{2...) while((s32[]{:T(128)}, f32[32,32,256]{2,1,0:T(8,128)S(1)}, ...), condition=%wide.region_7.9_spmd.clone, body=%wide.region_6.8_spmd.clone.sunk | while | flops 226821696 | bytes 5509559 | solution.py:29
  356.5 3.6 fusion.135
  363.8 3.6 fusion.135
  371.0 3.6 fusion.135
  378.3 3.6 fusion.135
  385.3 75.6 %reduce-scatter.9.cloned.1.call-done = f32[32,512]{1,0:T(8,128)} async-done(((f32[32,8192]{1,0:T(8,128)}), f32[32,512]{1,0:T(8,128)}) %reduce-scatter.9.cloned.1.call-update) | async-done | bytes 65552 | tf_op jit(solution)/shard_map/reduce_scatter | solution.py:49
  462.8 119.6 %all-gather.15.cloned.1.call-done = f32[8192,32]{1,0:T(8,128)} async-done(((f32[32,32]{1,0:T(8,128)}), f32[8192,32]{1,0:T(8,128)}) %all-gather.15.cloned.1.call-update) | async-done | bytes 1048592 | tf_op jit(solution)/shard_map/all_gather | solution.py:63
  582.5 2.5 reduce_sum.11
  585.1 2.9 cholesky.16
  592.8 36.1 %all-gather.13.cloned.1.call-done = f32[32,8192]{1,0:T(8,128)} async-done(((f32[32,512]{1,0:T(8,128)}), f32[32,8192]{1,0:T(8,128)}) %all-gather.13.cloned.1.call-update) | async-done | bytes 1048592 | tf_op jit(solution)/shard_map/all_gather | solution.py:46
  630.3 23.8 %while.47 = (s32[]{:T(128)}, f32[32,32,256]{2,1,0:T(8,128)S(1)}, s32[]{:T(128)}, f32[32,256,256]{2,1,0:T(8,128)}, s32[32]{0:T(128)S(1)}, /*index=5*/f32[32,32,25...) while((s32[]{:T(128)}, f32[32,32,256]{2,1,0:T(8,128)S(1)}, ...), condition=%wide.region_13.15_spmd.clone, body=%wide.region_12.14_spmd.clone.sunk | while | flops 226821696 | bytes 5509559 | solution.py:29
  631.6 3.6 fusion.141
  637.6 3.6 fusion.141
  643.5 3.6 fusion.141
  649.5 3.6 fusion.141
  655.7 75.7 %reduce-scatter.11.cloned.1.call-done = f32[32,512]{1,0:T(8,128)} async-done(((f32[32,8192]{1,0:T(8,128)}), f32[32,512]{1,0:T(8,128)}) %reduce-scatter.11.cloned.1.call-update) | async-done | bytes 65552 | tf_op jit(solution)/shard_map/reduce_scatter | solution.py:49
  732.4 77.3 %psum.7 = f32[32,32]{1,0:T(8,128)S(1)} all-reduce(f32[32,32]{1,0:T(8,128)S(1)} %fusion.80), channel_id=1, replica_groups=mesh['row'=16,'col'=16] {'row','col'}, use_global_device_ids=true, to_apply=%region_15.17 | all-reduce | flops 1024 | bytes 8192 | tf_op jit(solution)/shard_map/psum | solution.py:68
  (140 shorter events, 76.6 us)
Async XLA Ops:
  7.2 45.4 %all-gather.7.cloned.1.call-start = ((), (), s32[]{:S(2)}) async-start(), calls=%async_computation.4 | async-start | bytes 1114112 | tf_op jit(solution)/shard_map/all_gather | solution.py:46
  7.9 152.5 %reduce-scatter.5.cloned.1.call-start = ((), (), s32[]{:S(2)}) async-start(), calls=%async_computation.5 | async-start | bytes 1114112 | tf_op jit(solution)/shard_map/reduce_scatter | solution.py:49
  54.1 106.3 %copy-start = (f32[32,512]{1,0:T(8,128)S(1)}, f32[32,512]{1,0:T(8,128)}, u32[]{:S(2)}) copy-start(f32[32,512]{1,0:T(8,128)} %param.16) | copy-start | bytes 196612
  54.1 106.3 %copy-start.5 = (f32[512]{0:T(512)S(1)}, f32[512]{0:T(512)}, u32[]{:S(2)}) copy-start(f32[512]{0:T(512)} %param.17) | copy-start | bytes 6148
  84.8 118.2 %all-gather.9.cloned.1.call-start = ((), (), s32[]{:S(2)}) async-start(), calls=%async_computation.6 | async-start | bytes 1114112 | tf_op jit(solution)/shard_map/all_gather | solution.py:46
  161.9 148.8 %reduce-scatter.7.cloned.1.call-start = ((), (), s32[]{:S(2)}) async-start(), calls=%async_computation.7 | async-start | bytes 1114112 | tf_op jit(solution)/shard_map/reduce_scatter | solution.py:49
  204.4 106.3 %copy-start.2 = (f32[32,512]{1,0:T(8,128)S(1)}, f32[32,512]{1,0:T(8,128)}, u32[]{:S(2)}) copy-start(f32[32,512]{1,0:T(8,128)} %reduce-scatter.5.cloned.1.call-done) | copy-start | bytes 196612
  235.0 118.0 %all-gather.11.cloned.1.call-start = ((), (), s32[]{:S(2)}) async-start(), calls=%async_computation.8 | async-start | bytes 1114112 | tf_op jit(solution)/shard_map/all_gather | solution.py:46
  312.3 148.7 %reduce-scatter.9.cloned.1.call-start = ((), (), s32[]{:S(2)}) async-start(), calls=%async_computation.9 | async-start | bytes 1114112 | tf_op jit(solution)/shard_map/reduce_scatter | solution.py:49
  354.5 106.4 %copy-start.3 = (f32[32,512]{1,0:T(8,128)S(1)}, f32[32,512]{1,0:T(8,128)}, u32[]{:S(2)}) copy-start(f32[32,512]{1,0:T(8,128)} %multiply_subtract_fusion.1) | copy-start | bytes 196612
  383.6 246.7 %copy-start.4 = (s32[32]{0:T(128)S(1)}, s32[32]{0:T(128)}, u32[]{:S(2)}) copy-start(s32[32]{0:T(128)} %get-tuple-element.843) | copy-start | bytes 388
  383.6 246.7 %copy-start.6 = (s32[32]{0:T(128)S(1)}, s32[32]{0:T(128)}, u32[]{:S(2)}) copy-start(s32[32]{0:T(128)} %get-tuple-element.851) | copy-start | bytes 388
  385.2 197.3 %all-gather.15.cloned.1.call-start = ((), (), s32[]{:S(2)}) async-start(), calls=%async_computation.12 | async-start | bytes 4210688 | tf_op jit(solution)/shard_map/all_gather | solution.py:63
  462.6 166.2 %all-gather.13.cloned.1.call-start = ((), (), s32[]{:S(2)}) async-start(), calls=%async_computation.10 | async-start | bytes 1114112 | tf_op jit(solution)/shard_map/all_gather | solution.py:46
  592.7 138.7 %reduce-scatter.11.cloned.1.call-start = ((), (), s32[]{:S(2)}) async-start(), calls=%async_computation.11 | async-start | bytes 1114112 | tf_op jit(solution)/shard_map/reduce_scatter | solution.py:49
  630.3 101.1 %copy-start.1 = (f32[32,512]{1,0:T(8,128)S(1)}, f32[32,512]{1,0:T(8,128)}, u32[]{:S(2)}) copy-start(f32[32,512]{1,0:T(8,128)} %fusion.87) | copy-start | bytes 196612
Sparse Core Ops, SparseCore 0:
  9.8 42.7 all-gather.6
  84.9 75.4 reduce-scatter.4
  162.8 40.0 all-gather.8
  235.2 75.5 reduce-scatter.6
  313.0 40.0 all-gather.10
  385.3 75.5 reduce-scatter.8
  465.2 117.2 all-gather.14
  592.8 35.9 all-gather.12
  655.8 75.5 reduce-scatter.10
